TPU v7x, 32 devices: a whole 2x2x4 slice. The times are simulated.
32 devices in a mesh: sta: 4 (over y, x), evt: 8 (over z, core).
Axes of the slice: x: 2, y: 2, z: 4, core: 2. Of those that a mesh axis runs over, the one named last changes fastest.
Arguments:
- traces: bfloat16 [3, 32, 512, 2048], P(None, 'sta', 'evt'), may hold values from -96 to 96
- baz_bin: int32 [32, 512], P('sta', 'evt'), may hold values from 0 to 35
- inc_bin: int32 [32, 512], P('sta', 'evt'), may hold values from 0 to 7
- counts: int32 [32], P('sta'), may hold values from 64 to 512
- depth_index: int32 [32, 512], P('sta'), may hold values from 0 to 2046
- tile_of: int32 [32], replicated, may hold values from 0 to 15
Outputs:
- stack: float32 [16, 5, 2, 512], P('sta', None, None, 'evt')
All inputs are finite; a program needn't handle non-finite values.
Results may differ from a plain program's by a relative error of at most 0.0003.
Values sent between devices are 32-bit elements; how exact they have to be, the bound alone decides.
A program may use at most 64 MiB of HBM per device.

v0:
```python
import jax
import jax.numpy as jnp
from jax import lax
from jax.sharding import PartitionSpec as P

NS = 2048
DEPTHS = 512
BAZ_BINS = 36
TILE_DEV = 4


def solve_blocks(normal, right):
    factor = jnp.linalg.cholesky(normal)
    middle = jax.scipy.linalg.solve_triangular(factor, right, lower=True)
    return jax.scipy.linalg.solve_triangular(factor, middle, lower=True, trans=1)


def to_depths(values, indices):
    picks = indices[:, None, None, :]
    first = jnp.take_along_axis(values, picks, axis=3)
    second = jnp.take_along_axis(values, picks + 1, axis=3)
    return 0.5 * (first + second)


def body(traces, baz_bin, inc_bin, counts, depth_index, tile_of):
    highest = lax.Precision.HIGHEST
    stations = traces.shape[1]
    slots = traces.shape[2]
    evt_count = lax.axis_size("evt")
    depth_share = DEPTHS // evt_count
    phi = (baz_bin.astype(jnp.float32) + 0.5) * (2.0 * jnp.pi / BAZ_BINS)
    incidence = (12.0 + 2.5 * (inc_bin.astype(jnp.float32) + 0.5)) * (jnp.pi / 180.0)
    cosine = jnp.cos(phi)[:, :, None]
    sine = jnp.sin(phi)[:, :, None]
    vertical = traces[0].astype(jnp.float32)
    north = traces[1].astype(jnp.float32)
    east = traces[2].astype(jnp.float32)
    radial = -(cosine * north + sine * east)
    quality = jnp.cos(incidence)[:, :, None] * radial + jnp.sin(incidence)[:, :, None] * vertical
    transverse = sine * north - cosine * east
    data = jnp.concatenate([quality, transverse], axis=2)
    slot_ids = lax.axis_index("evt") * slots + jnp.arange(slots)
    live = (slot_ids[None, :] < counts[:, None]).astype(jnp.float32)
    harm = jnp.stack(
        [jnp.ones_like(phi), jnp.cos(phi), jnp.sin(phi), jnp.cos(2.0 * phi), jnp.sin(2.0 * phi)],
        axis=2,
    )
    weighted = harm * live[:, :, None]
    normal_part = jnp.einsum("sek,sel->skl", weighted, harm, precision=highest)
    rhs_part = jnp.einsum("sek,sec->skc", weighted, data, precision=highest)
    normal = lax.psum(normal_part, "evt") + jnp.eye(5, dtype=jnp.float32)[None]
    shares = lax.psum_scatter(rhs_part, "evt", scatter_dimension=2, tiled=True)
    solved = solve_blocks(normal, shares)
    coeff = lax.all_gather(solved, "evt", axis=2, tiled=True).reshape(stations, 5, 2, NS)
    mine = lax.dynamic_slice_in_dim(
        depth_index, lax.axis_index("evt") * depth_share, depth_share, 1
    )
    profile = to_depths(coeff, mine)
    first_tile = lax.axis_index("sta") * TILE_DEV
    own_tiles = first_tile + jnp.arange(TILE_DEV)
    members = jnp.sum((tile_of[None, :] == own_tiles[:, None]).astype(jnp.float32), axis=1)
    everyone = lax.all_gather(profile, "sta", axis=0, tiled=True)
    onehot = (tile_of[None, :] == own_tiles[:, None]).astype(jnp.float32)
    sums = jnp.einsum("ts,skcz->tkcz", onehot, everyone, precision=highest)
    return sums / jnp.maximum(members, 1.0)[:, None, None, None]


def solution(mesh):
    return jax.shard_map(
        body,
        mesh=mesh,
        in_specs=(
            P(None, "sta", "evt", None),
            P("sta", "evt"),
            P("sta", "evt"),
            P("sta"),
            P("sta", None),
            P(),
        ),
        out_specs=P("sta", None, None, "evt"),
        check_vma=False,
    )
```

profile of v0, /device:TPU:0, one launch (start us, length us, event | category | flops | bytes accessed | tf_op | source)
XLA Modules:
  0.0 130.2 jit_solution(14801742810654873437)
XLA Ops:
  6.5 0.0 reduce-scatter.2.cloned.1.call-start
  6.5 0.8 fusion.24
  7.3 0.7 compare_convert_fusion
  8.0 6.8 %fusion.7 = (f32[8,64,2048]{2,1,0:T(8,128)}, f32[8,64,2048]{2,1,0:T(8,128)}) fusion(bf16[3,8,64,2048]{3,2,1,0:T(8,128)(2,1)} %param.8, f32[8,64]{1,0:T(8,128)S(1)} %get-tuple-element.18, f32[8,64]{1,0:T(8,128)S(1)} %get-tuple-element.13, f32[8,64]{1,0:T(8,128)S(1)} %get-tuple-element.15, f32[8,64]{1,0:T(8,128)S(1)} %get-tuple-element.19), kind=kLoop, calls=%fused_computation.13 | loop fusion | flops 13631488 | bytes 14688256 | tf_op jit(solution)/shard_map/add | solution.py:39
  14.9 0.0 copy-start
  14.9 0.0 copy-start.1
  14.9 7.3 %fusion = f32[8,5,4096]{2,1,0:T(8,128)} fusion(f32[8,64,2048]{2,1,0:T(8,128)} %get-tuple-element.7, f32[8,64,2048]{2,1,0:T(8,128)} %get-tuple-element.6, f32[8,64,5]{1,2,0:T(8,128)S(1)} %stack.19, f32[8,64]{1,0:T(8,128)S(1)} %compare_convert_fusion), kind=kOutput, calls=%fused_computation.2 | convolution fusion | flops 127928832 | bytes 9056256 | tf_op jit(solution)/shard_map/sek,sec->skc/dot_general | solution.py:50
  22.2 0.0 reduce-scatter.2.cloned.1.call-update
  22.2 0.2 fusion.10
  22.4 30.3 %psum.7 = f32[8,5,5]{1,2,0:T(8,128)S(1)} all-reduce(f32[8,5,5]{1,2,0:T(8,128)S(1)} %fusion.10), channel_id=1, replica_groups=mesh['sta'=4,'evt'=8] {'evt'}, use_global_device_ids=true, to_apply=%region_0.0 | all-reduce | flops 200 | bytes 1600 | tf_op jit(solution)/shard_map/psum | solution.py:51
  52.8 0.1 copy.30
  52.9 0.1 copy.31
  53.0 3.7 %custom-call.11 = f32[8,5,5]{2,1,0:T(8,128)S(1)} custom-call(f32[8,5,5]{2,1,0:T(8,128)S(1)} %fusion.17), custom_call_target="Cholesky" | custom-call | tf_op jit(solution)/shard_map/jit(cholesky)/cholesky | solution.py:13
  56.7 0.1 compare_reduce_fusion
  56.9 0.1 select_bitcast_fusion
  56.9 3.2 %custom-call.12 = f32[8,1,5,5]{2,3,1,0:T(8,128)S(1)} custom-call(f32[8,1,5,5]{3,2,1,0:T(8,128)S(1)} %select_bitcast_fusion), custom_call_target="InvertDiagBlocksLowerTriangular" | custom-call | tf_op jit(solution)/shard_map/jit(_solve_triangular)/vmap()/triangular_solve | solution.py:15
  60.1 0.0 copy-done
  60.1 0.1 bitcast_or_fusion.1
  60.2 0.1 reshape.123
  60.3 0.1 reshape.128
  60.4 0.1 and_bitcast_fusion.1
  60.5 0.0 copy-done.1
  60.5 0.2 fusion.28
  60.7 0.0 reduce-scatter.2.cloned.1.call-done
  60.7 1.2 fusion.15
  61.9 0.3 fusion.13
  62.2 16.4 %all_gather.6 = f32[8,5,4096]{2,1,0:T(8,128)S(1)} all-gather(f32[8,5,512]{2,1,0:T(8,128)S(1)} %fusion.13), channel_id=1, replica_groups=mesh['sta'=4,'evt'=8] {'evt'}, dimensions={2}, use_global_device_ids=true | all-gather | bytes 737280 | tf_op jit(solution)/shard_map/all_gather | solution.py:54
  78.5 0.6 reshape.133
  79.1 17.0 %copy.34 = f32[8,5,2,2048]{1,2,3,0:T(2,128)} copy(f32[8,5,2,2048]{3,2,1,0:T(2,128)S(1)} %reshape.133) | data formatting | bytes 1310720 | tf_op jit(solution)/shard_map/reshape | solution.py:54
  96.1 8.3 %gather_fusion = f32[512,5,2]{1,2,0:T(2,128)S(1)} fusion(f32[8,5,2,2048]{1,2,3,0:T(2,128)} %copy.34, s32[512]{0:T(512)S(1)} %reshape.123), kind=kCustom, calls=%fused_computation.clone | custom fusion | bytes 45056 | tf_op jit(solution)/shard_map/jit(take_along_axis)/gather | solution.py:20
  104.4 0.2 copy.44
  104.6 8.3 %gather_fusion.1 = f32[512,5,2]{1,2,0:T(2,128)S(1)} fusion(f32[8,5,2,2048]{1,2,3,0:T(2,128)} %copy.34, s32[512]{0:T(512)S(1)} %reshape.128), kind=kCustom, calls=%fused_computation.1.clone | custom fusion | bytes 45056 | tf_op jit(solution)/shard_map/jit(take_along_axis)/gather | solution.py:21
  113.0 0.2 copy.46
  113.2 9.3 %all_gather.7 = f32[32,5,2,64]{3,0,2,1:T(8,128)S(1)} all-gather(f32[8,5,2,64]{3,0,2,1:T(8,128)S(1)} %fusion.12), channel_id=1, replica_groups=mesh['sta'=4,'evt'=8] {'sta'}, dimensions={0}, use_global_device_ids=true | all-gather | bytes 102400 | tf_op jit(solution)/shard_map/all_gather | solution.py:62
  122.6 0.2 convolution_divide_fusion
  122.8 0.6 copy.38
  (12 shorter events, 0.1 us)
Async XLA Ops:
  6.5 54.2 %reduce-scatter.2.cloned.1.call-start = ((), (), s32[]{:S(2)}) async-start(), calls=%async_computation.1 | async-start | bytes 1179648 | tf_op jit(solution)/shard_map/reduce_scatter | solution.py:52
  14.9 45.2 %copy-start = (s32[8,512]{1,0:T(8,128)S(1)}, s32[8,512]{1,0:T(8,128)}, u32[]{:S(2)}) copy-start(s32[8,512]{1,0:T(8,128)} %param.12) | copy-start | bytes 49156
  14.9 45.6 %copy-start.1 = (s32[32]{0:T(128)S(1)}, s32[32]{0:T(128)}, u32[]{:S(2)}) copy-start(s32[32]{0:T(128)} %param.13) | copy-start | bytes 388
Sparse Core Ops, SparseCore 0:
  22.3 35.4 reduce-scatter.1
where the time goes:
time: 131 us; the launch traced here: 130 us
  blocking collectives  56 us (43%)
  local copies, waits for them, and re-layouts  35.7 us (27%)
  other arithmetic  15.8 us (12%)
  between operations  13.5 us (10%)
  matrix products  9.13 us (7%)
    psum x1, blocking collectives, body(): normal = lax.psum(normal_part, 'evt') + jnp.eye(5, dtype=jnp.float32)[None]  30.3 us
    reshape x2, local copies, waits for them, and re-layouts, body(): lax.all_gather(solved, 'evt', axis=2, tiled=True)  17.5 us
    all_gather x1, blocking collectives, body(): lax.all_gather(solved, 'evt', axis=2, tiled=True)  16.4 us
    all_gather x1, blocking collectives, body(): everyone = lax.all_gather(profile, 'sta', axis=0, tiled=True)  9.34 us
    gather x3, local copies, waits for them, and re-layouts, to_depths(): second = jnp.take_along_axis(values, picks + 1, axis=3)  8.62 us
    gather x3, local copies, waits for them, and re-layouts, to_depths(): first = jnp.take_along_axis(values, picks, axis=3)  8.62 us
    dot_general x1, matrix products, body(): rhs_part = jnp.einsum('sek,sec->skc', weighted, data, precision=highest)  7.27 us
    add x1, other arithmetic, body(): jnp.cos(incidence)[:, :, None] * radial  6.81 us
  transfers between devices with their start and end apart: 1, of which 0 were waited for; matrix products, arithmetic and copies ran while one was open for 6% of the time, Pallas kernels for 0%

commit v1 on v0

--- a/solution.py
+++ b/solution.py
@@ -23,6 +23,23 @@
 
 
 def body(traces, baz_bin, inc_bin, counts, depth_index, tile_of):
+
+    def follow_cubes_here(xs, mine_x):
+        link_axis = "sta"
+        even, earlier, row_out = (
+            jax.lax.psum(1, link_axis),
+            jax.lax.axis_index(link_axis),
+            xs.shape[0],
+        )
+        history = list(map(lambda kk: (kk, (kk + 1) % even), range(even)))
+        carry_out, z1 = (xs, None)
+        for it in tuple(range(even)):
+            kept_arr = jax.lax.ppermute(carry_out, link_axis, history) if it < even - 1 else None
+            local_part = mine_x(carry_out, (earlier - it) % even * row_out)
+            z1 = local_part if z1 is None else z1 + local_part
+            carry_out = kept_arr
+        return z1
+
     highest = lax.Precision.HIGHEST
     stations = traces.shape[1]
     slots = traces.shape[2]
@@ -59,9 +76,16 @@
     first_tile = lax.axis_index("sta") * TILE_DEV
     own_tiles = first_tile + jnp.arange(TILE_DEV)
     members = jnp.sum((tile_of[None, :] == own_tiles[:, None]).astype(jnp.float32), axis=1)
-    everyone = lax.all_gather(profile, "sta", axis=0, tiled=True)
     onehot = (tile_of[None, :] == own_tiles[:, None]).astype(jnp.float32)
-    sums = jnp.einsum("ts,skcz->tkcz", onehot, everyone, precision=highest)
+    sums = follow_cubes_here(
+        profile,
+        lambda part, start: jnp.einsum(
+            "ts,skcz->tkcz",
+            lax.dynamic_slice_in_dim(onehot, start, part.shape[0], axis=1),
+            part,
+            precision=highest,
+        ),
+    )
     return sums / jnp.maximum(members, 1.0)[:, None, None, None]
 
 

time: 131 us -> 136 us (1.038)
  waiting for transfers between devices: 0.04 us -> 12 us
  blocking collectives: 56 us -> 47 us
  starting transfers between devices: 0.01 us -> 2.13 us
    ppermute x0 -> x3, waiting for transfers between devices: none -> 12 us  [follow_cubes_here(): jax.lax.ppermute(carry_out, link_axis, history)]
    all_gather x1 -> x0, blocking collectives: 9.34 us -> none  [body(): everyone = lax.all_gather(profile, 'sta', axis=0, tiled=True)]
    ppermute x0 -> x3, starting transfers between devices: none -> 2.12 us  [follow_cubes_here(): jax.lax.ppermute(carry_out, link_axis, history)]
  transfers between devices with their start and end apart: 1 -> 4, of which waited for: 0 -> 3; matrix products, arithmetic and copies ran while one was open for 6% -> 6% of each run, Pallas kernels for 0% -> 0%
where the time goes in v1:
time: 136 us
  blocking collectives  47 us (35%)
  local copies, waits for them, and re-layouts  35.7 us (26%)
  other arithmetic  15.8 us (12%)
  between operations  13.6 us (10%)
  waiting for transfers between devices  12 us (9%)
  matrix products  9.76 us (7%)
  starting transfers between devices  2.13 us (2%)
    psum x1, blocking collectives, body(): normal = lax.psum(normal_part, 'evt') + jnp.eye(5, dtype=jnp.float32)[None]  30.6 us
    reshape x2, local copies, waits for them, and re-layouts, body(): lax.all_gather(solved, 'evt', axis=2, tiled=True)  17.5 us
    all_gather x1, blocking collectives, body(): lax.all_gather(solved, 'evt', axis=2, tiled=True)  16.4 us
    ppermute x3, waiting for transfers between devices, follow_cubes_here(): jax.lax.ppermute(carry_out, link_axis, history)  12 us
    gather x3, local copies, waits for them, and re-layouts, to_depths(): second = jnp.take_along_axis(values, picks + 1, axis=3)  8.62 us
    gather x3, local copies, waits for them, and re-layouts, to_depths(): first = jnp.take_along_axis(values, picks, axis=3)  8.62 us
    dot_general x1, matrix products, body(): rhs_part = jnp.einsum('sek,sec->skc', weighted, data, precision=highest)  7.27 us
    add x1, other arithmetic, body(): jnp.cos(incidence)[:, :, None] * radial  6.81 us
  transfers between devices with their start and end apart: 4, of which 3 were waited for; matrix products, arithmetic and copies ran while one was open for 6% of the time, Pallas kernels for 0%

profile of v1, /device:TPU:0, one launch (start us, length us, event | category | flops | bytes accessed | tf_op | source)
XLA Modules:
  0.0 136.0 jit_solution(9164463858901650917)
XLA Ops:
  6.5 0.0 reduce-scatter.2.cloned.1.call-start
  6.5 0.8 fusion.25
  7.3 0.7 compare_convert_fusion
  8.0 6.8 %fusion.7 = (f32[8,64,2048]{2,1,0:T(8,128)}, f32[8,64,2048]{2,1,0:T(8,128)}) fusion(bf16[3,8,64,2048]{3,2,1,0:T(8,128)(2,1)} %param.8, f32[8,64]{1,0:T(8,128)S(1)} %get-tuple-element.20, f32[8,64]{1,0:T(8,128)S(1)} %get-tuple-element.15, f32[8,64]{1,0:T(8,128)S(1)} %get-tuple-element.17, f32[8,64]{1,0:T(8,128)S(1)} %get-tuple-element.21), kind=kLoop, calls=%fused_computation.13 | loop fusion | flops 13631488 | bytes 14688256 | tf_op jit(solution)/shard_map/add | solution.py:56
  14.9 0.0 copy-start
  14.9 0.0 copy-start.1
  14.9 7.3 %fusion = f32[8,5,4096]{2,1,0:T(8,128)} fusion(f32[8,64,2048]{2,1,0:T(8,128)} %get-tuple-element.9, f32[8,64,2048]{2,1,0:T(8,128)} %get-tuple-element.8, f32[8,64,5]{1,2,0:T(8,128)S(1)} %stack.19, f32[8,64]{1,0:T(8,128)S(1)} %compare_convert_fusion), kind=kOutput, calls=%fused_computation.2 | convolution fusion | flops 127928832 | bytes 9056256 | tf_op jit(solution)/shard_map/sek,sec->skc/dot_general | solution.py:67
  22.2 0.0 reduce-scatter.2.cloned.1.call-update
  22.2 0.2 fusion.11
  22.5 30.6 %psum.7 = f32[8,5,5]{1,2,0:T(8,128)S(1)} all-reduce(f32[8,5,5]{1,2,0:T(8,128)S(1)} %fusion.11), channel_id=1, replica_groups=mesh['sta'=4,'evt'=8] {'evt'}, use_global_device_ids=true, to_apply=%region_0.0 | all-reduce | flops 200 | bytes 1600 | tf_op jit(solution)/shard_map/psum | solution.py:68
  53.1 0.1 copy.30
  53.2 0.1 copy.31
  53.4 3.7 %custom-call.11 = f32[8,5,5]{2,1,0:T(8,128)S(1)} custom-call(f32[8,5,5]{2,1,0:T(8,128)S(1)} %fusion.18), custom_call_target="Cholesky" | custom-call | tf_op jit(solution)/shard_map/jit(cholesky)/cholesky | solution.py:13
  57.1 0.1 compare_reduce_fusion
  57.2 0.1 select_bitcast_fusion
  57.3 3.2 %custom-call.12 = f32[8,1,5,5]{2,3,1,0:T(8,128)S(1)} custom-call(f32[8,1,5,5]{3,2,1,0:T(8,128)S(1)} %select_bitcast_fusion), custom_call_target="InvertDiagBlocksLowerTriangular" | custom-call | tf_op jit(solution)/shard_map/jit(_solve_triangular)/vmap()/triangular_solve | solution.py:15
  60.5 0.0 copy-done
  60.5 0.1 bitcast_or_fusion.1
  60.6 0.1 reshape.123
  60.7 0.1 reshape.128
  60.7 0.1 and_bitcast_fusion.1
  60.8 0.0 copy-done.1
  60.8 0.2 convert_reduce_fusion
  61.0 0.0 reduce-scatter.2.cloned.1.call-done
  61.0 1.2 fusion.16
  62.3 0.3 fusion.14
  62.5 16.4 %all_gather.3 = f32[8,5,4096]{2,1,0:T(8,128)S(1)} all-gather(f32[8,5,512]{2,1,0:T(8,128)S(1)} %fusion.14), channel_id=1, replica_groups=mesh['sta'=4,'evt'=8] {'evt'}, dimensions={2}, use_global_device_ids=true | all-gather | bytes 737280 | tf_op jit(solution)/shard_map/all_gather | solution.py:71
  78.9 0.6 reshape.136
  79.4 17.0 %copy.34 = f32[8,5,2,2048]{1,2,3,0:T(2,128)} copy(f32[8,5,2,2048]{3,2,1,0:T(2,128)S(1)} %reshape.136) | data formatting | bytes 1310720 | tf_op jit(solution)/shard_map/reshape | solution.py:71
  96.4 8.3 %gather_fusion = f32[512,5,2]{1,2,0:T(2,128)S(1)} fusion(f32[8,5,2,2048]{1,2,3,0:T(2,128)} %copy.34, s32[512]{0:T(512)S(1)} %reshape.123), kind=kCustom, calls=%fused_computation.clone | custom fusion | bytes 45056 | tf_op jit(solution)/shard_map/jit(take_along_axis)/gather | solution.py:20
  104.7 0.2 copy.47
  105.0 8.3 %gather_fusion.1 = f32[512,5,2]{1,2,0:T(2,128)S(1)} fusion(f32[8,5,2,2048]{1,2,3,0:T(2,128)} %copy.34, s32[512]{0:T(512)S(1)} %reshape.128), kind=kCustom, calls=%fused_computation.1.clone | custom fusion | bytes 45056 | tf_op jit(solution)/shard_map/jit(take_along_axis)/gather | solution.py:21
  113.3 0.2 copy.49
  113.6 1.5 %collective-permute-start = (f32[8,5,2,64]{3,0,2,1:T(8,128)S(1)}, f32[8,5,2,64]{3,0,2,1:T(8,128)S(1)}, u32[]{:S(2)}, u32[]{:S(2)}) collective-permute-start(f32[8,5,2,64]{3,0,2,1:T(8,128)S(1)} %fusion.13), channel_id=1, source_target_pairs={{0,8},{8,16},{16,24},{24,0},{1,9},{9,17},{17,25},{25,1},{2,10},{10... | collective-permute-start | bytes 61448 | tf_op jit(solution)/shard_map/ppermute | solution.py:37
  115.1 0.2 fusion.32
  115.3 3.2 %collective-permute-done = f32[8,5,2,64]{3,0,2,1:T(8,128)S(1)} collective-permute-done((f32[8,5,2,64]{3,0,2,1:T(8,128)S(1)}, f32[8,5,2,64]{3,0,2,1:T(8,128)S(1)}, u32[]{:S(2)}, u32[]{:S(2)}) %collective-permute-start) | collective-permute-done | bytes 20512 | tf_op jit(solution)/shard_map/ppermute | solution.py:37
  118.5 0.6 collective-permute-start.1
  119.1 0.2 convolution_add_fusion.2
  119.3 4.1 %collective-permute-done.1 = f32[8,5,2,64]{3,0,2,1:T(8,128)S(1)} collective-permute-done((f32[8,5,2,64]{3,0,2,1:T(8,128)S(1)}, f32[8,5,2,64]{3,0,2,1:T(8,128)S(1)}, u32[]{:S(2)}, u32[]{:S(2)}) %collective-permute-start.1) | collective-permute-done | bytes 20512 | tf_op jit(solution)/shard_map/ppermute | solution.py:37
  123.4 0.0 collective-permute-start.2
  123.4 0.2 convolution_add_fusion.1
  123.6 4.7 %collective-permute-done.2 = f32[8,5,2,64]{3,0,2,1:T(8,128)S(1)} collective-permute-done((f32[8,5,2,64]{3,0,2,1:T(8,128)S(1)}, f32[8,5,2,64]{3,0,2,1:T(8,128)S(1)}, u32[]{:S(2)}, u32[]{:S(2)}) %collective-permute-start.2) | collective-permute-done | bytes 20512 | tf_op jit(solution)/shard_map/ppermute | solution.py:37
  128.3 0.2 fusion.9
  128.5 0.6 copy.38
  (12 shorter events, 0.1 us)
Async XLA Ops:
  6.5 54.5 %reduce-scatter.2.cloned.1.call-start = ((), (), s32[]{:S(2)}) async-start(), calls=%async_computation.1 | async-start | bytes 1179648 | tf_op jit(solution)/shard_map/reduce_scatter | solution.py:69
  14.9 45.6 %copy-start = (s32[8,512]{1,0:T(8,128)S(1)}, s32[8,512]{1,0:T(8,128)}, u32[]{:S(2)}) copy-start(s32[8,512]{1,0:T(8,128)} %param.12) | copy-start | bytes 49156
  14.9 45.9 %copy-start.1 = (s32[32]{0:T(128)S(1)}, s32[32]{0:T(128)}, u32[]{:S(2)}) copy-start(s32[32]{0:T(128)} %param.13) | copy-start | bytes 388
  113.6 5.0 %collective-permute-start = (f32[8,5,2,64]{3,0,2,1:T(8,128)S(1)}, f32[8,5,2,64]{3,0,2,1:T(8,128)S(1)}, u32[]{:S(2)}, u32[]{:S(2)}) collective-permute-start(f32[8,5,2,64]{3,0,2,1:T(8,128)S(1)} %fusion.13), channel_id=1, source_target_pairs={{0,8},{8,16},{16,24},{24,0},{1,9},{9,17},{17,25},{25,1},{2,10},{10... | collective-permute-start | bytes 61448 | tf_op jit(solution)/shard_map/ppermute | solution.py:37
  118.5 4.9 %collective-permute-start.1 = (f32[8,5,2,64]{3,0,2,1:T(8,128)S(1)}, f32[8,5,2,64]{3,0,2,1:T(8,128)S(1)}, u32[]{:S(2)}, u32[]{:S(2)}) collective-permute-start(f32[8,5,2,64]{3,0,2,1:T(8,128)S(1)} %collective-permute-done), channel_id=1, source_target_pairs={{0,8},{8,16},{16,24},{24,0},{1,9},{9,17},{17,25},{25,1},{2,10},{10... | collective-permute-start | bytes 61448 | tf_op jit(solution)/shard_map/ppermute | solution.py:37
  123.4 4.9 %collective-permute-start.2 = (f32[8,5,2,64]{3,0,2,1:T(8,128)S(1)}, f32[8,5,2,64]{3,0,2,1:T(8,128)S(1)}, u32[]{:S(2)}, u32[]{:S(2)}) collective-permute-start(f32[8,5,2,64]{3,0,2,1:T(8,128)S(1)} %collective-permute-done.1), channel_id=1, source_target_pairs={{0,8},{8,16},{16,24},{24,0},{1,9},{9,17},{17,25},{25,1},{2,10},{10... | collective-permute-start | bytes 61448 | tf_op jit(solution)/shard_map/ppermute | solution.py:37
Sparse Core Ops, SparseCore 0:
  22.3 35.3 reduce-scatter.1
